TPU v7x, 32 devices: a whole 2x2x4 slice. The times are simulated.
32 devices in a mesh: tm: 4 (over x, core), cell: 8 (over z, y).
Axes of the slice: x: 2, y: 2, z: 4, core: 2. Of those that a mesh axis runs over, the one named last changes fastest.
Arguments:
- sensitivity: bfloat16 [2048, 4, 4096], P(None, 'tm', 'cell'), may hold values from -0.1875 to 0.1875
- duals: bfloat16 [2048, 128], P(('tm', 'cell')), may hold values from -6 to 6
- time_cov: float32 [4, 4], replicated, may hold values from 0.05 to 0.5
- cell_coords: int32 [2, 4096], P(None, 'cell'), may hold values from 0 to 127, as said below
- obs_time: int32 [2048], replicated, may hold values from 0 to 3
- obs_owner: int32 [2048], replicated, may hold values from 0 to 2047, each once
Outputs:
- product: float32 [2048, 128], P(('tm', 'cell'))
Inputs may be any that keep to these rules, and one draw needn't show every extreme that they name: `cell_coords`: every cell has its own grid position; rows lie below 32 and columns below 128. `obs_owner`: every observation stands in exactly one slot.
All inputs are finite; a program needn't handle non-finite values.
Results may differ from a plain program's by a relative error of at most 0.0049.
Values may be sent and summed in bfloat16 or wider, within the bound.
A program may use at most 64 MiB of HBM per device.

v0:
```python
import jax
import jax.numpy as jnp
from jax import lax
from jax.sharding import PartitionSpec as P

LSCALE = 4


def covariance(left_coords, right_coords):
    row_gap = (left_coords[0][:, None] - right_coords[0][None, :]).astype(jnp.float32)
    col_gap = (left_coords[1][:, None] - right_coords[1][None, :]).astype(jnp.float32)
    distance = jnp.sqrt(row_gap * row_gap + col_gap * col_gap)
    return (jnp.exp(-distance / LSCALE) / (8.0 * LSCALE)).astype(jnp.bfloat16)


def per_device(sensitivity, duals, time_cov, cell_coords, obs_time, obs_owner):
    obs_count = sensitivity.shape[0]
    time_count = sensitivity.shape[1]
    cell_count = sensitivity.shape[2]
    real_count = duals.shape[1]
    first_time = lax.axis_index("tm") * time_count
    time_index = first_time + jnp.arange(time_count, dtype=jnp.int32)
    live = time_index[None, :, None] <= obs_time[:, None, None]
    masked = jnp.where(live, sensitivity, jnp.zeros((), jnp.bfloat16))
    flattened = masked.reshape(obs_count, time_count * cell_count)
    picked = flattened
    adjoint = lax.dot_general(
        picked,
        lax.all_gather(duals, ("tm", "cell"), axis=0, tiled=True),
        (((0,), (0,)), ((), ())),
        preferred_element_type=jnp.float32,
    )
    local_adj = (
        adjoint.astype(jnp.bfloat16).reshape(time_count, cell_count, real_count).transpose(1, 0, 2)
    )
    all_coords = lax.all_gather(cell_coords, "cell", axis=1, tiled=True)
    cov_rows = lax.dynamic_slice_in_dim(time_cov, first_time, time_count, 0)
    mixed = jnp.einsum(
        "st,ctr->csr",
        cov_rows,
        lax.all_gather(local_adj, "tm", axis=1, tiled=True).astype(jnp.float32),
        precision=lax.Precision.HIGHEST,
    ).astype(jnp.bfloat16)
    portion = lax.all_gather(mixed, "cell", axis=0, tiled=True)
    kernel = covariance(cell_coords, all_coords)
    summed = jnp.dot(
        kernel, portion.reshape(portion.shape[0], -1), preferred_element_type=jnp.float32
    )
    weighted = summed.reshape(mixed.shape).astype(jnp.bfloat16)
    weighted_flat = weighted.transpose(1, 0, 2).reshape(time_count * cell_count, real_count)
    picked = jnp.take(flattened, obs_owner, axis=0)
    return lax.psum_scatter(
        jnp.dot(picked, weighted_flat, preferred_element_type=jnp.float32),
        ("tm", "cell"),
        scatter_dimension=0,
        tiled=True,
    )


def solution(mesh):
    in_specs = (P(None, "tm", "cell"), P(("tm", "cell"), None), P(), P(None, "cell"), P(), P())
    out_specs = P(("tm", "cell"), None)
    return jax.shard_map(
        per_device, mesh=mesh, in_specs=in_specs, out_specs=out_specs, check_vma=False
    )
```

profile of v0, /device:TPU:0, one launch (start us, length us, event | category | flops | bytes accessed | tf_op | source)
XLA Modules:
  0.0 281.4 jit_solution(13908487538062645309)
XLA Ops:
  6.5 0.0 copy-start
  6.5 0.0 all-gather.4.cloned.1.call-start
  6.5 0.7 broadcast_compare_fusion
  7.3 72.8 %all_gather.13 = bf16[2048,128]{1,0:T(8,128)(2,1)S(1)} all-gather(bf16[64,128]{1,0:T(8,128)(2,1)} %param.7), channel_id=1, replica_groups=mesh['tm'=4,'cell'=8] {'tm','cell'}, dimensions={0}, use_global_device_ids=true | all-gather | bytes 540672 | tf_op jit(solution)/shard_map/all_gather | solution.py:29
  80.1 1.8 select_bitcast_fusion
  81.9 0.8 convolution_convert_fusion
  82.6 0.0 copy-start.1
  82.6 6.8 %all-gather = bf16[512,512]{1,0:T(8,128)(2,1)S(1)} all-gather(bf16[512,128]{1,0:T(8,128)(2,1)S(1)} %convolution_convert_fusion), channel_id=2, replica_groups=mesh['tm'=4,'cell'=8] {'tm'}, dimensions={1}, use_global_device_ids=true | all-gather | bytes 655360 | tf_op jit(solution)/shard_map/all_gather | solution.py:41
  89.5 0.1 reshape.40
  89.6 0.0 copy-done
  89.6 1.0 fusion.7
  90.6 0.7 convert_element_type.27
  91.3 0.0 all-gather.4.cloned.1.call-update
  91.3 0.0 reduce-scatter.2.cloned.1.call-start
  91.3 0.0 copy-done.1
  91.3 0.0 copy-start.2
  91.4 9.2 %gather_fusion = bf16[2048,512]{1,0:T(8,128)(2,1)} fusion(bf16[2048,512]{1,0:T(8,128)(2,1)S(1)} %select_bitcast_fusion, s32[2048]{0:T(1024)S(1)} %fusion.6), kind=kCustom, calls=%fused_computation | custom fusion | bytes 4202496 | tf_op jit(solution)/shard_map/jit(_take)/gather | solution.py:51
  100.6 0.0 copy-done.2
  100.6 30.7 %all_gather.12 = s32[2,4096]{1,0:T(2,128)S(1)} all-gather(s32[2,512]{1,0:T(2,128)S(1)} %copy-done.2), channel_id=1, replica_groups=mesh['tm'=4,'cell'=8] {'cell'}, dimensions={1}, use_global_device_ids=true | all-gather | bytes 36864 | tf_op jit(solution)/shard_map/all_gather | solution.py:36
  131.3 0.0 all-gather.4.cloned.1.call-done
  131.3 9.2 %fusion.1 = f32[2048,128]{1,0:T(8,128)} fusion(bf16[2048,512]{1,0:T(8,128)(2,1)} %gather_fusion, pred[2048]{0:T(1024)(128)(4,1)S(1)} %compare_and_fusion, bf16[4096,128]{1,0:T(8,128)(2,1)} %all-gather.4.cloned.1.call-done, s32[4096]{0:T(1024)S(1)} %bitcast.19, s32[512]{0:T(512)S(1)} %bitcast.21, s32[4096]{0:T(1024)S(1)} %bitcast.18, s32[512]{0:T(512)S(1)} %bitcast.20), kind=kOutput, calls=%fused_computation.3 | convolution fusion | flops 829489152 | bytes 4233216 | tf_op jit(solution)/shard_map/dot_general | solution.py:53
  140.5 0.0 reduce-scatter.2.cloned.1.call-update
  140.5 134.1 %reduce-scatter.2.cloned.1.call-done = f32[64,128]{1,0:T(8,128)} async-done(((f32[2048,128]{1,0:T(8,128)}), f32[64,128]{1,0:T(8,128)}) %reduce-scatter.2.cloned.1.call-update) | async-done | bytes 32784 | tf_op jit(solution)/shard_map/reduce_scatter | solution.py:52
  (4 shorter events, 0.0 us)
Async XLA Ops:
  6.5 83.1 %copy-start = (f32[4,4]{1,0:T(4,128)S(1)}, f32[4,4]{1,0:T(4,128)}, u32[]{:S(2)}) copy-start(f32[4,4]{1,0:T(4,128)} %param.8) | copy-start | bytes 196
  6.5 124.8 %all-gather.4.cloned.1.call-start = ((), (), s32[]{:S(2)}) async-start(), calls=%async_computation.2 | async-start | bytes 1179648 | tf_op jit(solution)/shard_map/all_gather | solution.py:44
  82.6 8.7 %copy-start.1 = (s32[2048]{0:T(1024)S(1)}, s32[2048]{0:T(1024)}, u32[]{:S(2)}) copy-start(s32[2048]{0:T(1024)} %param.11) | copy-start | bytes 24580
  91.3 183.3 %reduce-scatter.2.cloned.1.call-start = ((), (), s32[]{:S(2)}) async-start(), calls=%async_computation.1 | async-start | bytes 1081344 | tf_op jit(solution)/shard_map/reduce_scatter | solution.py:52
  91.3 9.2 %copy-start.2 = (s32[2,512]{1,0:T(2,128)S(1)}, s32[2,512]{1,0:T(2,128)}, u32[]{:S(2)}) copy-start(s32[2,512]{1,0:T(2,128)} %param.9) | copy-start | bytes 12292
Sparse Core Ops, SparseCore 0:
  91.4 37.0 all-gather.3
  140.6 133.8 reduce-scatter.1
where the time goes:
time: 282 us; the launch traced here: 281 us
  waiting for transfers between devices  134 us (48%)
  blocking collectives  110 us (39%)
  between operations  13.5 us (5%)
  matrix products  10.9 us (4%)
  local copies, waits for them, and re-layouts  9.39 us (3%)
  other arithmetic  3.15 us (1%)
    reduce_scatter x1, waiting for transfers between devices, per_device(): lax.psum_scatter(jnp.dot(picked, weighted_flat, preferred_element_type=jn...  134 us
    all_gather x1, blocking collectives, per_device(): lax.all_gather(duals, ('tm', 'cell'), axis=0, tiled=True)  72.8 us
    all_gather x1, blocking collectives, per_device(): all_coords = lax.all_gather(cell_coords, 'cell', axis=1, tiled=True)  30.7 us
    gather x1, local copies, waits for them, and re-layouts, per_device(): picked = jnp.take(flattened, obs_owner, axis=0)  9.22 us
    dot_general x1, matrix products, per_device(): jnp.dot(picked, weighted_flat, preferred_element_type=jnp.float32)  9.15 us
    all_gather x1, blocking collectives, per_device(): lax.all_gather(local_adj, 'tm', axis=1, tiled=True).astype(jnp.float32)  6.83 us
  transfers between devices with their start and end apart: 2, of which 1 were waited for; matrix products, arithmetic and copies ran while one was open for 3% of the time, Pallas kernels for 0%

commit v1 on v0

v1 whole, which is shorter than its diff:
```python
import functools

import jax
import jax.numpy as jnp
from jax import lax
from jax.experimental import pallas as pl
from jax.experimental.pallas import tpu as pltpu
from jax.sharding import PartitionSpec as P

LSCALE = 4
LANES = 128
HALVES = 2
PICK_ROWS = 256
MESH = pl.DeviceIdType.MESH
BF16 = jnp.bfloat16
F32 = jnp.float32


def remote(src, dst, sems, index, device):
    send, recv = sems
    return pltpu.make_async_remote_copy(
        src_ref=src, dst_ref=dst, send_sem=send.at[index], recv_sem=recv.at[index],
        device_id=device, device_id_type=MESH,
    )


def column_of(row):
    return jnp.broadcast_to(row, (LANES, row.shape[1])).T


def kernel(cfg, sens_hbm, duals_ref, cov_ref, coords_ref, time_ref, owner_ref, out_ref, *s):
    n_hi, n_cell, gather, scatter = cfg
    n_tm = 2 * n_hi
    (sens, full, coords_all, mask_t, picked, row_b, col_b, own_b, ids, cov_k, adj, held, acc,
     core_out, core_in, x_out, x_in, total, cell_out, cell_in, local_sem, *pairs) = s
    co, ac, ax, ap, bx, bp, ring_r, ring_l, dp, dx, dc = zip(pairs[0::2], pairs[1::2])
    obs, cells = sens.shape
    rows = duals_ref.shape[0]
    half = cells // HALVES

    tm = lax.axis_index("tm")
    cell = lax.axis_index("cell")
    hi, core = tm // 2, tm % 2
    partner = (hi * 2 + (1 - core), cell)

    def hi_at(q):
        return lax.rem(hi + q + n_hi, n_hi)

    def x_peer(q):
        return (hi_at(q) * 2 + core, cell)

    def cell_at(k):
        return lax.rem(cell + k + n_cell, n_cell)

    load = pltpu.make_async_copy(sens_hbm, sens, local_sem)
    load.start()

    barrier = pltpu.get_barrier_semaphore()
    peers = [(tm, cell_at(k)) for k in range(1, n_cell)] + [x_peer(q) for q in range(1, n_hi)] + [partner]
    for peer in peers:
        pl.semaphore_signal(barrier, inc=1, device_id=peer, device_id_type=MESH)
    pl.semaphore_wait(barrier, len(peers))

    sent = []

    def go(copy):
        copy.start()
        sent.append(copy)
        return copy

    co_copies = {}
    for k in range(1, n_cell):
        co_copies[k] = go(remote(coords_ref, coords_all.at[cell], co, k, (tm, cell_at(k))))

    def block(t, c):
        return full.at[t * n_cell + c]

    cell_copies, x_copies, core_copies = {}, {}, {}

    def forward_x(src, k):
        for q in range(1, n_hi):
            x_copies[q, k] = go(remote(src, block(tm, cell_at(-k)), ax, q * n_cell + k, x_peer(q)))

    def forward_core(src, q, k):
        dst = block(hi_at(-q) * 2 + core, cell_at(-k))
        core_copies[q, k] = go(remote(src, dst, ap, q * n_cell + k, partner))

    if gather:
        for k in range(1, n_cell):
            cell_copies[k] = go(remote(duals_ref, block(tm, cell), ac, k, (tm, cell_at(k))))
        forward_x(duals_ref, 0)
        forward_core(duals_ref, 0, 0)
        full[tm * n_cell + cell] = duals_ref[...]

    coords_all[cell] = coords_ref[...]
    row_b[...] = column_of(coords_ref[0:1, :].astype(F32))
    col_b[...] = column_of(coords_ref[1:2, :].astype(F32))
    own_b[...] = column_of(owner_ref[...].astype(F32))
    live = tm <= time_ref[...]
    ids[...] = jnp.where(live, lax.broadcasted_iota(jnp.int32, (1, obs), 1), -1).astype(F32)

    def covariance_block(k):
        c = cell_at(-k)

        @pl.loop(0, cells // LANES)
        def _(j):
            lanes = pl.ds(pl.multiple_of(j * LANES, LANES), LANES)
            row_gap = row_b[...] - coords_all[c, 0:1, lanes].astype(F32)
            col_gap = col_b[...] - coords_all[c, 1:2, lanes].astype(F32)
            distance = jnp.sqrt(row_gap * row_gap + col_gap * col_gap)
            cov_k[c, :, lanes] = (jnp.exp(-distance / LSCALE) / (8.0 * LSCALE)).astype(BF16)

    def pick(i):
        at = slice(i * PICK_ROWS, (i + 1) * PICK_ROWS)
        owned = own_b[at, :]
        hot = [
            jnp.where(owned == ids[:, j * LANES:(j + 1) * LANES], 1.0, 0.0).astype(BF16)
            for j in range(obs // LANES)
        ]
        picked[at, :] = jnp.dot(
            jnp.concatenate(hot, axis=1), sens[...], preferred_element_type=F32
        ).astype(BF16)

    fillers = [functools.partial(pick, i) for i in range(obs // PICK_ROWS)]

    def fill():
        if fillers:
            fillers.pop(0)()

    covariance_block(0)
    load.wait()

    @pl.loop(0, obs // PICK_ROWS)
    def _(i):
        at = pl.ds(pl.multiple_of(i * PICK_ROWS, PICK_ROWS), PICK_ROWS)
        alive = jnp.where(ids[:, at] >= 0.0, 1.0, 0.0).astype(BF16)
        mask_t[:, at] = sens[at, :].T * alive

    for k in range(1, n_cell):
        if gather:
            cell_copies[k].wait_recv()
            src = block(tm, cell_at(-k))
            forward_x(src, k)
            forward_core(src, 0, k)
    if gather:
        for k in range(n_cell):
            for q in range(1, n_hi):
                x_copies[q, k].wait_recv()
                forward_core(block(hi_at(-q) * 2 + core, cell_at(-k)), q, k)
    for k in range(1, n_cell):
        co_copies[k].wait_recv()
        if k <= n_cell // 2:
            covariance_block(k)
    if gather:
        for k in range(n_cell):
            for q in range(n_hi):
                core_copies[q, k].wait_recv()

    bx_copies, bp_copies = {}, {}
    for h in range(HALVES):
        at = slice(h * half, (h + 1) * half)
        everything = full[...].reshape(obs, LANES) if gather else duals_ref[...]
        adj[tm, at, :] = jnp.dot(mask_t[at, :], everything, preferred_element_type=F32).astype(BF16)
        here = adj.at[tm, at]
        for q in range(1, n_hi):
            bx_copies[q, h] = go(remote(here, here, bx, q * HALVES + h, x_peer(q)))
        bp_copies[0, h] = go(remote(here, here, bp, h, partner))

    for k in range(n_cell // 2 + 1, n_cell):
        covariance_block(k)
    for h in range(HALVES):
        for q in range(1, n_hi):
            bx_copies[q, h].wait_recv()
            got = adj.at[hi_at(-q) * 2 + core, h * half:(h + 1) * half]
            bp_copies[q, h] = go(remote(got, got, bp, q * HALVES + h, partner))
    fill()

    major = cell // 2
    place = jnp.where(cell % 2 == 0, major, n_cell - 1 - major)

    def cell_on(k):
        p = lax.rem(place + k + n_cell, n_cell)
        return jnp.where(p < n_cell // 2, p * 2, (n_cell - 1 - p) * 2 + 1)

    steps = n_cell // 2
    ring = {}

    def carries(way, step, h):
        return step < steps or (step == steps and (h == 0 if way > 0 else h == 1))

    def ring_send(way, step, h):
        if carries(way, step, h):
            part = held.at[cell_on(-way * (step - 1)), h * half:(h + 1) * half]
            sems = ring_r if way > 0 else ring_l
            ring[way, step, h] = go(remote(part, part, sems, step * HALVES + h, (tm, cell_on(way))))

    for h in range(HALVES):
        at = slice(h * half, (h + 1) * half)
        for q in range(n_hi):
            bp_copies[q, h].wait_recv()
        mixed = cov_ref[tm, 0] * adj[0, at, :].astype(F32)
        for t in range(1, n_tm):
            mixed += cov_ref[tm, t] * adj[t, at, :].astype(F32)
        held[cell, at, :] = mixed.astype(BF16)
        ring_send(1, 1, h)
        ring_send(-1, 1, h)

    def spread(c):
        return jnp.dot(cov_k[c], held[c], preferred_element_type=F32)

    acc[...] = spread(cell)
    for step in range(1, steps + 1):
        for h in range(HALVES):
            for way in (1, -1):
                if carries(way, step, h):
                    ring[way, step, h].wait_recv()
                    ring_send(way, step + 1, h)
            fill()
        if step < steps:
            acc[...] += spread(cell_on(-step)) + spread(cell_on(step))
        else:
            acc[...] += spread(cell_on(step))
    while fillers:
        fill()

    weighted = acc[...].astype(BF16)
    if scatter:
        span = rows * n_cell

        def product(t):
            at = pl.ds(pl.multiple_of(t * span, span), span)
            return jnp.dot(picked[at, :], weighted, preferred_element_type=F32)

        dp_copies, dx_copies, dc_copies = {}, {}, {}
        order = [*range(1, n_hi), 0]
        for q in order:
            core_out[q] = product(hi_at(q) * 2 + (1 - core)).astype(BF16)
            dp_copies[q] = go(remote(core_out.at[q], core_in.at[q], dp, q, partner))
        for q in order:
            summed = product(hi_at(q) * 2 + core)
            dp_copies[q].wait_recv()
            summed += core_in[q].astype(F32)
            if q:
                x_out[q] = summed.astype(BF16)
                dx_copies[q] = go(remote(x_out.at[q], x_in.at[q], dx, q, x_peer(q)))
        for q in range(1, n_hi):
            dx_copies[q].wait_recv()
            summed += x_in[q].astype(F32)
        total[...] = summed.reshape(n_cell, rows, LANES)
        cell_out[...] = summed.astype(BF16).reshape(n_cell, rows, LANES)
        for k in range(1, n_cell):
            dc_copies[k] = go(remote(cell_out.at[cell_at(k)], cell_in.at[k], dc, k, (tm, cell_at(k))))
        result = total[cell]
        for k in range(1, n_cell):
            dc_copies[k].wait_recv()
            result += cell_in[k].astype(F32)
        out_ref[...] = result
    else:
        for i in range(obs // PICK_ROWS):
            at = slice(i * PICK_ROWS, (i + 1) * PICK_ROWS)
            out_ref[at, :] = jnp.dot(picked[at, :], weighted, preferred_element_type=F32)

    for copy in sent:
        copy.wait_send()


def per_device(n_tm, n_cell, sensitivity, duals, time_cov, cell_coords, obs_time, obs_owner):
    obs, _, cells = sensitivity.shape
    rows, reals = duals.shape
    n_hi = n_tm // 2
    inside = rows % 16 == 0
    if not inside:
        duals = lax.all_gather(duals, ("tm", "cell"), axis=0, tiled=True)
    span = rows * n_cell if inside else 16
    part = rows if inside else 16
    vmem = pl.BlockSpec(memory_space=pltpu.VMEM)

    def pair(count):
        return [pltpu.SemaphoreType.DMA((count,)), pltpu.SemaphoreType.DMA((count,))]

    steps = n_cell // 2 + 1
    out_rows = rows if inside else obs
    out = pl.pallas_call(
        functools.partial(kernel, (n_hi, n_cell, inside, inside)),
        out_shape=jax.ShapeDtypeStruct((out_rows, reals), F32),
        in_specs=[
            pl.BlockSpec(memory_space=pl.ANY), vmem, pl.BlockSpec(memory_space=pltpu.SMEM), vmem, vmem, vmem,
        ],
        out_specs=vmem,
        scratch_shapes=[
            pltpu.VMEM((obs, cells), BF16),
            pltpu.VMEM((n_tm * n_cell if inside else 1, part, reals), BF16),
            pltpu.VMEM((n_cell, 2, cells), jnp.int32),
            pltpu.VMEM((cells, obs), BF16),
            pltpu.VMEM((obs, cells), BF16),
            pltpu.VMEM((cells, LANES), F32),
            pltpu.VMEM((cells, LANES), F32),
            pltpu.VMEM((obs, LANES), F32),
            pltpu.VMEM((1, obs), F32),
            pltpu.VMEM((n_cell, cells, cells), BF16),
            pltpu.VMEM((n_tm, cells, reals), BF16),
            pltpu.VMEM((n_cell, cells, reals), BF16),
            pltpu.VMEM((cells, reals), F32),
            pltpu.VMEM((n_hi, span, reals), BF16),
            pltpu.VMEM((n_hi, span, reals), BF16),
            pltpu.VMEM((n_hi, span, reals), BF16),
            pltpu.VMEM((n_hi, span, reals), BF16),
            pltpu.VMEM((n_cell, part, reals), F32),
            pltpu.VMEM((n_cell, part, reals), BF16),
            pltpu.VMEM((n_cell, part, reals), BF16),
            pltpu.SemaphoreType.DMA,
            *pair(n_cell), *pair(n_cell), *pair(n_hi * n_cell), *pair(n_hi * n_cell),
            *pair(n_hi * HALVES), *pair(n_hi * HALVES),
            *pair(steps * HALVES), *pair(steps * HALVES),
            *pair(n_hi), *pair(n_hi), *pair(n_cell),
        ],
        compiler_params=pltpu.CompilerParams(
            collective_id=0, has_side_effects=True, vmem_limit_bytes=62 * 1024 * 1024
        ),
    )(
        sensitivity.reshape(obs, cells), duals, time_cov, cell_coords,
        obs_time.reshape(1, obs), obs_owner.reshape(1, obs),
    )
    if inside:
        return out
    return lax.psum_scatter(out, ("tm", "cell"), scatter_dimension=0, tiled=True)


def solution(mesh):
    in_specs = (P(None, "tm", "cell"), P(("tm", "cell"), None), P(), P(None, "cell"), P(), P())
    out_specs = P(("tm", "cell"), None)
    return jax.shard_map(
        functools.partial(per_device, mesh.shape["tm"], mesh.shape["cell"]),
        mesh=mesh, in_specs=in_specs, out_specs=out_specs, check_vma=False,
    )
```

time: 282 us -> 54.7 us (0.19)
  waiting for transfers between devices: 134 us -> 0 us
  blocking collectives: 110 us -> 0 us
  Pallas kernels: 0 us -> 53.1 us
  between operations: 13.5 us -> 0.01 us
  matrix products: 10.9 us -> 0 us
  local copies, waits for them, and re-layouts: 9.39 us -> 1.38 us
  other arithmetic: 3.15 us -> 0 us
    reduce_scatter x1 -> x0, waiting for transfers between devices: 134 us -> none  [per_device(): lax.psum_scatter(jnp.dot(picked, weighted_flat, preferred_element_type=jn...]
    all_gather x3 -> x0, blocking collectives: 110 us -> none  [the longest x1 72.8 us: per_device(): lax.all_gather(duals, ('tm', 'cell'), axis=0, tiled=True)]
    pallas_call x0 -> x1, Pallas kernels: none -> 53.1 us  [per_device(): pl.pallas_call(functools.partial(kernel, (n_hi, n_cell, inside, inside)),...]
    dot_general x3 -> x0, matrix products: 10.9 us -> none  [the longest x1 9.15 us: per_device(): jnp.dot(picked, weighted_flat, preferred_element_type=jnp.float32)]
    gather x1 -> x0, local copies, waits for them, and re-layouts: 9.22 us -> none  [per_device(): picked = jnp.take(flattened, obs_owner, axis=0)]
  transfers between devices with their start and end apart: 2 -> 0, of which waited for: 1 -> 0; matrix products, arithmetic and copies ran while one was open for 3% -> 0% of each run, Pallas kernels for 0% -> 0%
where the time goes in v1:
time: 54.7 us; the launch traced here: 54.5 us
  Pallas kernels  53.1 us (97%)
  local copies, waits for them, and re-layouts  1.38 us (3%)
    pallas_call x1, Pallas kernels, per_device(): pl.pallas_call(functools.partial(kernel, (n_hi, n_cell, inside, inside)),...  53.1 us
    unnamed x1, local copies, waits for them, and re-layouts  1.38 us

profile of v1, /device:TPU:0, one launch (start us, length us, event | category | flops | bytes accessed | tf_op | source)
XLA Modules:
  0.0 54.5 jit_solution(7816829571591172519)
XLA Ops:
  0.0 53.1 %shard_map.64 = f32[64,128]{1,0:T(8,128)} custom-call(bf16[2048,512]{1,0:T(8,128)(2,1)} %bitcast.3, bf16[64,128]{1,0:T(8,128)(2,1)} %duals_ref.1, f32[4,4]{1,0:T(4,128)} %cov_ref.1, s32[2,512]{1,0:T(2,128)} %coords_ref.1, s32[1,2048]{1,0:T(1,128)} %bitcast.4, s32[1,2048]{1,0:T(1,128)} %bitcast.5), custom_call_target="tpu_custom_call" | custom-call | tf_op jit(solution)/shard_map/pallas_call | solution.py:283
  53.1 1.4 %copy.8 = f32[64,128]{1,0:T(8,128)} copy(f32[64,128]{1,0:T(8,128)} %shard_map.64) | data formatting | bytes 65536

commit v2 on v1

--- a/solution.py
+++ b/solution.py
@@ -11,6 +11,8 @@
 LANES = 128
 HALVES = 2
 PICK_ROWS = 256
+QUARTERS = 4
+FILL = (0, 3, 3, 1, 1)
 MESH = pl.DeviceIdType.MESH
 BF16 = jnp.bfloat16
 F32 = jnp.float32
@@ -37,6 +39,7 @@
     obs, cells = sens.shape
     rows = duals_ref.shape[0]
     half = cells // HALVES
+    quarter = cells // QUARTERS
 
     tm = lax.axis_index("tm")
     cell = lax.axis_index("cell")
@@ -59,39 +62,6 @@
     peers = [(tm, cell_at(k)) for k in range(1, n_cell)] + [x_peer(q) for q in range(1, n_hi)] + [partner]
     for peer in peers:
         pl.semaphore_signal(barrier, inc=1, device_id=peer, device_id_type=MESH)
-    pl.semaphore_wait(barrier, len(peers))
-
-    sent = []
-
-    def go(copy):
-        copy.start()
-        sent.append(copy)
-        return copy
-
-    co_copies = {}
-    for k in range(1, n_cell):
-        co_copies[k] = go(remote(coords_ref, coords_all.at[cell], co, k, (tm, cell_at(k))))
-
-    def block(t, c):
-        return full.at[t * n_cell + c]
-
-    cell_copies, x_copies, core_copies = {}, {}, {}
-
-    def forward_x(src, k):
-        for q in range(1, n_hi):
-            x_copies[q, k] = go(remote(src, block(tm, cell_at(-k)), ax, q * n_cell + k, x_peer(q)))
-
-    def forward_core(src, q, k):
-        dst = block(hi_at(-q) * 2 + core, cell_at(-k))
-        core_copies[q, k] = go(remote(src, dst, ap, q * n_cell + k, partner))
-
-    if gather:
-        for k in range(1, n_cell):
-            cell_copies[k] = go(remote(duals_ref, block(tm, cell), ac, k, (tm, cell_at(k))))
-        forward_x(duals_ref, 0)
-        forward_core(duals_ref, 0, 0)
-        full[tm * n_cell + cell] = duals_ref[...]
-
     coords_all[cell] = coords_ref[...]
     row_b[...] = column_of(coords_ref[0:1, :].astype(F32))
     col_b[...] = column_of(coords_ref[1:2, :].astype(F32))
@@ -99,9 +69,7 @@
     live = tm <= time_ref[...]
     ids[...] = jnp.where(live, lax.broadcasted_iota(jnp.int32, (1, obs), 1), -1).astype(F32)
 
-    def covariance_block(k):
-        c = cell_at(-k)
-
+    def covariance_block(c):
         @pl.loop(0, cells // LANES)
         def _(j):
             lanes = pl.ds(pl.multiple_of(j * LANES, LANES), LANES)
@@ -123,11 +91,12 @@
 
     fillers = [functools.partial(pick, i) for i in range(obs // PICK_ROWS)]
 
-    def fill():
-        if fillers:
-            fillers.pop(0)()
-
-    covariance_block(0)
+    def fill(count):
+        for _ in range(count):
+            if fillers:
+                fillers.pop(0)()
+
+    covariance_block(cell)
     load.wait()
 
     @pl.loop(0, obs // PICK_ROWS)
@@ -136,12 +105,48 @@
         alive = jnp.where(ids[:, at] >= 0.0, 1.0, 0.0).astype(BF16)
         mask_t[:, at] = sens[at, :].T * alive
 
+    fill(FILL[0])
+    pl.semaphore_wait(barrier, len(peers))
+
+    sent = []
+
+    def go(copy):
+        copy.start()
+        sent.append(copy)
+        return copy
+
+    co_copies = {}
+    for k in range(1, n_cell):
+        co_copies[k] = go(remote(coords_ref, coords_all.at[cell], co, k, (tm, cell_at(k))))
+
+    def block(t, c):
+        return full.at[t * n_cell + c]
+
+    cell_copies, x_copies, core_copies = {}, {}, {}
+
+    def forward_x(src, k):
+        for q in range(1, n_hi):
+            x_copies[q, k] = go(remote(src, block(tm, cell_at(-k)), ax, q * n_cell + k, x_peer(q)))
+
+    def forward_core(src, q, k):
+        dst = block(hi_at(-q) * 2 + core, cell_at(-k))
+        core_copies[q, k] = go(remote(src, dst, ap, q * n_cell + k, partner))
+
+    if gather:
+        for k in range(1, n_cell):
+            cell_copies[k] = go(remote(duals_ref, block(tm, cell), ac, k, (tm, cell_at(k))))
+        forward_x(duals_ref, 0)
+        forward_core(duals_ref, 0, 0)
+        full[tm * n_cell + cell] = duals_ref[...]
+
+    fill(FILL[1])
     for k in range(1, n_cell):
         if gather:
             cell_copies[k].wait_recv()
             src = block(tm, cell_at(-k))
             forward_x(src, k)
             forward_core(src, 0, k)
+    fill(FILL[2])
     if gather:
         for k in range(n_cell):
             for q in range(1, n_hi):
@@ -149,8 +154,6 @@
                 forward_core(block(hi_at(-q) * 2 + core, cell_at(-k)), q, k)
     for k in range(1, n_cell):
         co_copies[k].wait_recv()
-        if k <= n_cell // 2:
-            covariance_block(k)
     if gather:
         for k in range(n_cell):
             for q in range(n_hi):
@@ -166,14 +169,13 @@
             bx_copies[q, h] = go(remote(here, here, bx, q * HALVES + h, x_peer(q)))
         bp_copies[0, h] = go(remote(here, here, bp, h, partner))
 
-    for k in range(n_cell // 2 + 1, n_cell):
-        covariance_block(k)
+    fill(FILL[3])
     for h in range(HALVES):
         for q in range(1, n_hi):
             bx_copies[q, h].wait_recv()
             got = adj.at[hi_at(-q) * 2 + core, h * half:(h + 1) * half]
             bp_copies[q, h] = go(remote(got, got, bp, q * HALVES + h, partner))
-    fill()
+    fill(FILL[4])
 
     major = cell // 2
     place = jnp.where(cell % 2 == 0, major, n_cell - 1 - major)
@@ -186,14 +188,15 @@
     ring = {}
 
     def carries(way, step, h):
-        return step < steps or (step == steps and (h == 0 if way > 0 else h == 1))
+        return step < steps or (step == steps and (h < QUARTERS // 2) == (way > 0))
 
     def ring_send(way, step, h):
         if carries(way, step, h):
-            part = held.at[cell_on(-way * (step - 1)), h * half:(h + 1) * half]
+            part = held.at[cell_on(-way * (step - 1)), h * quarter:(h + 1) * quarter]
             sems = ring_r if way > 0 else ring_l
-            ring[way, step, h] = go(remote(part, part, sems, step * HALVES + h, (tm, cell_on(way))))
-
+            ring[way, step, h] = go(remote(part, part, sems, step * QUARTERS + h, (tm, cell_on(way))))
+
+    per_half = QUARTERS // HALVES
     for h in range(HALVES):
         at = slice(h * half, (h + 1) * half)
         for q in range(n_hi):
@@ -202,26 +205,30 @@
         for t in range(1, n_tm):
             mixed += cov_ref[tm, t] * adj[t, at, :].astype(F32)
         held[cell, at, :] = mixed.astype(BF16)
-        ring_send(1, 1, h)
-        ring_send(-1, 1, h)
+        for piece in range(h * per_half, (h + 1) * per_half):
+            ring_send(1, 1, piece)
+            ring_send(-1, 1, piece)
 
     def spread(c):
         return jnp.dot(cov_k[c], held[c], preferred_element_type=F32)
 
+    def blocks(step):
+        return [cell_on(-step), cell_on(step)] if step < steps else [cell_on(step)]
+
     acc[...] = spread(cell)
+    for c in blocks(1):
+        covariance_block(c)
     for step in range(1, steps + 1):
-        for h in range(HALVES):
+        for h in range(QUARTERS):
             for way in (1, -1):
                 if carries(way, step, h):
                     ring[way, step, h].wait_recv()
                     ring_send(way, step + 1, h)
-            fill()
-        if step < steps:
-            acc[...] += spread(cell_on(-step)) + spread(cell_on(step))
-        else:
-            acc[...] += spread(cell_on(step))
-    while fillers:
-        fill()
+            if step < steps and h < len(blocks(step + 1)):
+                covariance_block(blocks(step + 1)[h])
+        for c in blocks(step):
+            acc[...] += spread(c)
+    fill(len(fillers))
 
     weighted = acc[...].astype(BF16)
     if scatter:
@@ -236,21 +243,26 @@
         for q in order:
             core_out[q] = product(hi_at(q) * 2 + (1 - core)).astype(BF16)
             dp_copies[q] = go(remote(core_out.at[q], core_in.at[q], dp, q, partner))
+        far = sorted(range(n_cell), key=lambda k: -min(k, n_cell - k))
         for q in order:
             summed = product(hi_at(q) * 2 + core)
             dp_copies[q].wait_recv()
-            summed += core_in[q].astype(F32)
+            total[...] = (summed + core_in[q].astype(F32)).reshape(n_cell, rows, LANES)
             if q:
-                x_out[q] = summed.astype(BF16)
-                dx_copies[q] = go(remote(x_out.at[q], x_in.at[q], dx, q, x_peer(q)))
-        for q in range(1, n_hi):
-            dx_copies[q].wait_recv()
-            summed += x_in[q].astype(F32)
-        total[...] = summed.reshape(n_cell, rows, LANES)
-        cell_out[...] = summed.astype(BF16).reshape(n_cell, rows, LANES)
-        for k in range(1, n_cell):
-            dc_copies[k] = go(remote(cell_out.at[cell_at(k)], cell_in.at[k], dc, k, (tm, cell_at(k))))
-        result = total[cell]
+                for k in far:
+                    c = cell_at(k)
+                    x_out[q, c] = total[c].astype(BF16)
+                    dx_copies[q, k] = go(remote(x_out.at[q, c], x_in.at[q, c], dx, q * n_cell + k, x_peer(q)))
+        for k in far:
+            c = cell_at(k)
+            block_sum = total[c]
+            for q in range(1, n_hi):
+                dx_copies[q, k].wait_recv()
+                block_sum += x_in[q, c].astype(F32)
+            if k:
+                cell_out[c] = block_sum.astype(BF16)
+                dc_copies[k] = go(remote(cell_out.at[c], cell_in.at[k], dc, k, (tm, c)))
+        result = block_sum
         for k in range(1, n_cell):
             dc_copies[k].wait_recv()
             result += cell_in[k].astype(F32)
@@ -303,16 +315,16 @@
             pltpu.VMEM((cells, reals), F32),
             pltpu.VMEM((n_hi, span, reals), BF16),
             pltpu.VMEM((n_hi, span, reals), BF16),
-            pltpu.VMEM((n_hi, span, reals), BF16),
-            pltpu.VMEM((n_hi, span, reals), BF16),
+            pltpu.VMEM((n_hi, n_cell, part, reals), BF16),
+            pltpu.VMEM((n_hi, n_cell, part, reals), BF16),
             pltpu.VMEM((n_cell, part, reals), F32),
             pltpu.VMEM((n_cell, part, reals), BF16),
             pltpu.VMEM((n_cell, part, reals), BF16),
             pltpu.SemaphoreType.DMA,
             *pair(n_cell), *pair(n_cell), *pair(n_hi * n_cell), *pair(n_hi * n_cell),
             *pair(n_hi * HALVES), *pair(n_hi * HALVES),
-            *pair(steps * HALVES), *pair(steps * HALVES),
-            *pair(n_hi), *pair(n_hi), *pair(n_cell),
+            *pair(steps * QUARTERS), *pair(steps * QUARTERS),
+            *pair(n_hi), *pair(n_hi * n_cell), *pair(n_cell),
         ],
         compiler_params=pltpu.CompilerParams(
             collective_id=0, has_side_effects=True, vmem_limit_bytes=62 * 1024 * 1024

time: 54.7 us -> 51.7 us (0.945)
  Pallas kernels: 53.1 us -> 50 us
    pallas_call x1, Pallas kernels: 53.1 us -> 50 us  [per_device(): pl.pallas_call(functools.partial(kernel, (n_hi, n_cell, inside, inside)),...]
where the time goes in v2:
time: 51.7 us; the launch traced here: 51.4 us
  Pallas kernels  50 us (97%)
  local copies, waits for them, and re-layouts  1.38 us (3%)
    pallas_call x1, Pallas kernels, per_device(): pl.pallas_call(functools.partial(kernel, (n_hi, n_cell, inside, inside)),...  50 us
    unnamed x1, local copies, waits for them, and re-layouts  1.38 us

profile of v2, /device:TPU:0, one launch (start us, length us, event | category | flops | bytes accessed | tf_op | source)
XLA Modules:
  0.0 51.4 jit_solution(17254248384924954672)
XLA Ops:
  0.0 50.0 %shard_map.64 = f32[64,128]{1,0:T(8,128)} custom-call(bf16[2048,512]{1,0:T(8,128)(2,1)} %bitcast.3, bf16[64,128]{1,0:T(8,128)(2,1)} %duals_ref.1, f32[4,4]{1,0:T(4,128)} %cov_ref.1, s32[2,512]{1,0:T(2,128)} %coords_ref.1, s32[1,2048]{1,0:T(1,128)} %bitcast.4, s32[1,2048]{1,0:T(1,128)} %bitcast.5), custom_call_target="tpu_custom_call" | custom-call | tf_op jit(solution)/shard_map/pallas_call | solution.py:295
  50.1 1.4 %copy.8 = f32[64,128]{1,0:T(8,128)} copy(f32[64,128]{1,0:T(8,128)} %shard_map.64) | data formatting | bytes 65536
